TPU v7x, 128 devices: a whole 4x4x4 slice. The times are simulated.
128 devices in a mesh: wl: 32 (over x, y, core), tile: 4 (over z).
Axes of the slice: x: 4, y: 4, z: 4, core: 2. Of those that a mesh axis runs over, the one named last changes fastest.
Arguments:
- forward: float32 [128, 2, 1024, 1024], P(('wl', 'tile')), may hold values from -6 to 6
- adjoint: float32 [128, 2, 1024, 1024], P(('wl', 'tile')), may hold values from -6 to 6
- mode: float32 [2, 1024], replicated, may hold values from -6 to 6
- target: float32 [128], P(('wl', 'tile')), may hold values from 0 to 2
- wl_index: int32 [128], P(('wl', 'tile')), may hold values from 0 to 127, each once
- tile_of: int32 [128], replicated, may hold values from 0 to 127, each once
- density: float32 [1024, 1024], P(('wl', 'tile')), may hold values from 0 to 1
Outputs:
- gradient: float32 [1024, 1024], P(('wl', 'tile'))
All inputs are finite; a program needn't handle non-finite values.
Results may differ from a plain program's by a relative error of at most 0.00002.
Values sent between devices are 32-bit elements; how exact they have to be, the bound alone decides.
No kernel may reach another device: no remote copies, remote signals or barrier semaphores. Data moves between devices by JAX's collectives and lax.ppermute only.
A program may use at most 64 MiB of HBM per device.

v0:
```python
import jax
import jax.numpy as jnp
from jax import lax
from jax.sharding import Mesh
from jax.sharding import PartitionSpec as P

WL = ("wl_0", "wl_1", "wl_2")
WL_TILE = ("wl_0", "wl_1", "wl_2", "tile")


def cut_along(shard, dim, count):
    before, after = (shard.shape[:dim], shard.shape[dim + 1 :])
    return jnp.moveaxis(shard.reshape(*before, count, -1, *after), dim, 0)


def sum_at_owner(shard, axis, dim):
    blocks = cut_along(shard, dim, lax.axis_size(axis))
    arrived = lax.all_to_all(blocks, axis, split_axis=0, concat_axis=0, tiled=True)
    return arrived.sum(axis=0)


def sum_in_two_steps(shard, axes, dim):
    far, near = axes
    blocks = cut_along(shard, dim, lax.axis_size(far))
    nearer = sum_at_owner(blocks, near, dim + 1)
    arrived = lax.all_to_all(nearer, far, split_axis=0, concat_axis=0, tiled=True)
    return arrived.sum(axis=0)


def sent_to_all(shard, axis):
    copies = jnp.broadcast_to(shard, (lax.axis_size(axis), *shard.shape))
    return lax.all_to_all(copies, axis, split_axis=0, concat_axis=0, tiled=True)


def taken_together(shard, axis):
    everything = sent_to_all(shard, axis)
    return jnp.sum(everything, axis=0)


def by_axis(shard, axes):
    far, near = axes
    return taken_together(taken_together(shard, near), far)


def per_device(forward, adjoint, mode, target, wl_index, tile_of, density):
    wide = lax.axis_size(WL)
    narrow = lax.axis_size("tile")
    devices = wide * narrow
    rows = forward.shape[2]
    cols = forward.shape[3]
    fwd_re, fwd_im = (forward[0, 0], forward[0, 1])
    adj_re, adj_im = (adjoint[0, 0], adjoint[0, 1])
    mon = rows // 2
    over_re = jnp.sum(fwd_re[mon] * mode[0] - fwd_im[mon] * mode[1])
    over_im = jnp.sum(fwd_re[mon] * mode[1] + fwd_im[mon] * mode[0])
    fom = (over_re * over_re + over_im * over_im) / cols
    freq = 1.0 + wl_index[0].astype(jnp.float32) / devices
    field = freq * freq * (fwd_re * adj_re - fwd_im * adj_im)
    tile_rows = rows // devices
    total_fom = by_axis(fom, (("wl_0", "wl_1"), ("wl_2", "tile")))
    scale = total_fom / devices + 1.0
    weight = target[0] - fom / scale
    owned = sum_in_two_steps(
        (weight * field).reshape(devices, tile_rows, cols)[tile_of].reshape(rows, cols),
        (("wl_0", "wl_1"), ("wl_2", "tile")),
        0,
    )
    slope = 4.0 * (1.0 - jnp.tanh(4.0 * (density - 0.5)) ** 2)
    shaped = owned * slope
    squares = by_axis(jnp.sum(shaped * shaped), (("wl_0", "wl_1"), ("wl_2", "tile")))
    return shaped / jnp.sqrt(squares / (rows * cols) + 1e-06)


def solution(mesh):
    split = Mesh(
        mesh.devices.reshape(4, 4, 2, mesh.shape["tile"]), ("wl_0", "wl_1", "wl_2", "tile")
    )
    placed = (
        P(WL_TILE, None, None, None),
        P(WL_TILE, None, None, None),
        P(),
        P(WL_TILE),
        P(WL_TILE),
        P(),
        P(WL_TILE, None),
    )
    return jax.shard_map(
        per_device, mesh=split, in_specs=placed, out_specs=P(WL_TILE, None), check_vma=False
    )
```

profile of v0, /device:TPU:1, one launch (start us, length us, event | category | flops | bytes accessed | tf_op | source)
XLA Modules:
  0.0 142.1 jit_solution(17318965053689914151)
XLA Ops:
  0.0 0.8 fusion.1
  0.8 0.8 fusion
  1.6 0.7 add_reduce_fusion
  5.5 6.8 %all-to-all-start = ((f32[8,1,1]{2,1,0:T(1,128)}), f32[8,1,1]{2,1,0:T(1,128)S(1)}, u32[]{:S(2)}, u32[]{:S(2)}) async-start(f32[8,1,1]{2,1,0:T(1,128)} %broadcast_in_dim.15), calls=%async_computation | async-start | bytes 8192 | tf_op jit(solution)/shard_map/all_to_all | solution.py:32
  13.0 0.7 compare_select_fusion
  13.7 3.2 %all-to-all-done = f32[8,1,1]{2,1,0:T(1,128)S(1)} async-done(((f32[8,1,1]{2,1,0:T(1,128)}), f32[8,1,1]{2,1,0:T(1,128)S(1)}, u32[]{:S(2)}, u32[]{:S(2)}) %all-to-all-start) | async-done | bytes 64 | tf_op jit(solution)/shard_map/all_to_all | solution.py:32
  16.8 0.7 reduce_sum.83
  17.5 1.3 broadcast_in_dim.16
  18.8 6.8 %all-to-all-start.1 = ((f32[16,1,1]{2,1,0:T(1,128)}), f32[16,1,1]{2,1,0:T(1,128)S(1)}, u32[]{:S(2)}, u32[]{:S(2)}) async-start(f32[16,1,1]{2,1,0:T(1,128)} %broadcast_in_dim.16), calls=%async_computation.1 | async-start | bytes 16384 | tf_op jit(solution)/shard_map/all_to_all | solution.py:32
  26.2 5.7 %all-to-all-done.1 = f32[16,1,1]{2,1,0:T(1,128)S(1)} async-done(((f32[16,1,1]{2,1,0:T(1,128)}), f32[16,1,1]{2,1,0:T(1,128)S(1)}, u32[]{:S(2)}, u32[]{:S(2)}) %all-to-all-start.1) | async-done | bytes 96 | tf_op jit(solution)/shard_map/all_to_all | solution.py:32
  31.9 0.6 reduce_sum.84
  33.2 8.7 %multiply_bitcast_fusion = f32[128,8,1024]{2,1,0:T(8,128)} fusion(f32[1,2,1024,1024]{3,2,1,0:T(8,128)} %param.8, f32[1,2,1024,1024]{3,2,1,0:T(8,128)} %param.7, f32[]{:T(128)} %bitcast.5, f32[]{:T(128)S(6)} %sub.22), kind=kLoop, calls=%fused_computation.1 | loop fusion | flops 5242880 | bytes 20971528 | tf_op jit(solution)/shard_map/mul | solution.py:64
  42.0 5.0 %gather_fusion = f32[128,8,1024]{2,1,0:T(8,128)} fusion(f32[128,8,1024]{2,1,0:T(8,128)} %multiply_bitcast_fusion, s32[1024]{0:T(1024)S(1)} %pad_clamp_fusion), kind=kCustom, calls=%fused_computation | custom fusion | bytes 8389120 | tf_op jit(solution)/shard_map/gather | solution.py:64
  47.0 2.5 %copy.12 = f32[8,16,8,1024]{3,2,1,0:T(8,128)S(1)} copy(f32[8,16,8,1024]{3,2,0,1:T(8,128)} %bitcast.12) | data formatting | bytes 8388608 | tf_op jit(solution)/shard_map/transpose | solution.py:13
  49.4 54.0 %all_to_all.34 = f32[8,16,8,1024]{3,2,1,0:T(8,128)} all-to-all(f32[8,16,8,1024]{3,2,1,0:T(8,128)S(1)} %copy.12), channel_id=1, replica_groups=mesh['wl_0'=4,'wl_1'=4,'wl_2'=2,'tile'=4] {'wl_2','tile'}, dimensions={0} | all-to-all | bytes 8388608 | tf_op jit(solution)/shard_map/all_to_all | solution.py:18
  103.5 2.6 %reduce_sum.85 = f32[16,8,1024]{2,1,0:T(8,128)S(1)} reduce(f32[8,16,8,1024]{3,2,1,0:T(8,128)} %all_to_all.34, f32[]{:T(128)} %constant.7.clone.1), dimensions={0}, to_apply=%region_4.0 | reduce | flops 917504 | bytes 4718596 | tf_op jit(solution)/shard_map/reduce_sum | solution.py:19
  106.1 13.1 %all_to_all.35 = f32[16,8,1024]{2,1,0:T(8,128)S(1)} all-to-all(f32[16,8,1024]{2,1,0:T(8,128)S(1)} %reduce_sum.85), channel_id=1, replica_groups=mesh['wl_0'=4,'wl_1'=4,'wl_2'=2,'tile'=4] {'wl_0','wl_1'}, dimensions={0} | all-to-all | bytes 1048576 | tf_op jit(solution)/shard_map/all_to_all | solution.py:26
  119.2 0.6 multiply_reduce_fusion
  119.9 0.6 broadcast_in_dim.18
  120.5 9.0 %all_to_all.36 = f32[8,1,1]{2,1,0:T(1,128)S(1)} all-to-all(f32[8,1,1]{2,1,0:T(1,128)S(1)} %broadcast_in_dim.18), channel_id=1, replica_groups=mesh['wl_0'=4,'wl_1'=4,'wl_2'=2,'tile'=4] {'wl_2','tile'}, dimensions={0} | all-to-all | bytes 64 | tf_op jit(solution)/shard_map/all_to_all | solution.py:32
  130.1 0.6 broadcast_in_dim.19
  130.8 9.4 %all_to_all.37 = f32[16,1,1]{2,1,0:T(1,128)S(1)} all-to-all(f32[16,1,1]{2,1,0:T(1,128)S(1)} %broadcast_in_dim.19), channel_id=1, replica_groups=mesh['wl_0'=4,'wl_1'=4,'wl_2'=2,'tile'=4] {'wl_0','wl_1'}, dimensions={0} | all-to-all | bytes 128 | tf_op jit(solution)/shard_map/all_to_all | solution.py:32
  140.2 0.6 reduce_sum.89
  141.5 0.6 broadcast_divide_fusion
  (6 shorter events, 1.3 us)
Async XLA Ops:
  5.5 11.3 %all-to-all-start = ((f32[8,1,1]{2,1,0:T(1,128)}), f32[8,1,1]{2,1,0:T(1,128)S(1)}, u32[]{:S(2)}, u32[]{:S(2)}) async-start(f32[8,1,1]{2,1,0:T(1,128)} %broadcast_in_dim.15), calls=%async_computation | async-start | bytes 8192 | tf_op jit(solution)/shard_map/all_to_all | solution.py:32
  18.8 13.1 %all-to-all-start.1 = ((f32[16,1,1]{2,1,0:T(1,128)}), f32[16,1,1]{2,1,0:T(1,128)S(1)}, u32[]{:S(2)}, u32[]{:S(2)}) async-start(f32[16,1,1]{2,1,0:T(1,128)} %broadcast_in_dim.16), calls=%async_computation.1 | async-start | bytes 16384 | tf_op jit(solution)/shard_map/all_to_all | solution.py:32
  103.5 15.7 %copy-start = (f32[8,1024]{1,0:T(8,128)S(1)}, f32[8,1024]{1,0:T(8,128)}, u32[]{:S(2)}) copy-start(f32[8,1024]{1,0:T(8,128)} %param.13) | copy-start | bytes 98308
where the time goes:
time: 143 us; the launch traced here: 142 us
  blocking collectives  85.5 us (60%)
  other arithmetic  16.5 us (12%)
  starting transfers between devices  13.6 us (10%)
  local copies, waits for them, and re-layouts  12.2 us (9%)
  waiting for transfers between devices  8.85 us (6%)
  between operations  5.43 us (4%)
    all_to_all x1, blocking collectives, sum_at_owner(): lax.all_to_all(blocks, axis, split_axis=0, concat_axis=0, tiled=True)  54 us
    all_to_all x2, blocking collectives, sent_to_all(): return lax.all_to_all(copies, axis, split_axis=0, concat_axis=0, tiled=True)  18.4 us
    all_to_all x2, starting transfers between devices, sent_to_all(): return lax.all_to_all(copies, axis, split_axis=0, concat_axis=0, tiled=True)  13.6 us
    all_to_all x1, blocking collectives, sum_in_two_steps(): lax.all_to_all(nearer, far, split_axis=0, concat_axis=0, tiled=True)  13.1 us
    all_to_all x2, waiting for transfers between devices, sent_to_all(): return lax.all_to_all(copies, axis, split_axis=0, concat_axis=0, tiled=True)  8.85 us
    mul x1, other arithmetic, per_device(): weight * field  8.75 us
    gather x1, local copies, waits for them, and re-layouts, per_device(): (weight * field).reshape(devices, tile_rows, cols)[tile_of]  4.97 us
    broadcast_in_dim x4, local copies, waits for them, and re-layouts, sent_to_all(): copies = jnp.broadcast_to(shard, (lax.axis_size(axis), *shard.shape))  3.18 us
  transfers between devices with their start and end apart: 2, of which 2 were waited for; matrix products, arithmetic and copies ran while one was open for 0% of the time, Pallas kernels for 0%

commit v1 on v0

v1 whole, which is shorter than its diff:
```python
import functools

import jax
import jax.numpy as jnp
from jax import lax
from jax.experimental import pallas as pl
from jax.experimental.pallas import tpu as pltpu
from jax.sharding import Mesh
from jax.sharding import PartitionSpec as P

AXES = ("x", "y", "c", "z")
PLACES = ("x", "y", "z")
SIDE = 4
DEVICES = 128
STRIDE = {"x": 32, "y": 8, "z": 1}
CORE = 4
ROWS = 1024
COLS = 1024
TILE = 8
CUBE = 8
HALF = DEVICES // 2
CHUNK = 8
LANES = 128
MIB = 1 << 20

EVEN = ((0, 1), (2, 3))
ODD = ((0, 3), (1, 2))
FIRST = (EVEN, ODD)
SECOND = (ODD, EVEN)


def cubes(pairs_of_core):
    groups = []
    for core, pairs in enumerate(pairs_of_core):
        for px in pairs:
            for py in pairs:
                for pz in pairs:
                    groups.append(
                        [
                            STRIDE["x"] * x + STRIDE["y"] * y + CORE * core + z
                            for x in px
                            for y in py
                            for z in pz
                        ]
                    )
    return groups


def pair_member(place, odd, bit):
    if odd:
        low = jnp.minimum(place, SIDE - 1 - place)
        return (SIDE - 1 - low) if bit else low
    return (place // 2) * 2 + bit


def owner_parts(core):
    parts = {}
    for axis in PLACES:
        place = lax.axis_index(axis)
        table = []
        for k in (0, 1):
            for j in (0, 1):
                even_first = pair_member(pair_member(place, False, k), True, j)
                odd_first = pair_member(pair_member(place, True, k), False, j)
                chosen = jnp.where(core == 0, even_first, odd_first)
                table.append(chosen * STRIDE[axis])
        parts[axis] = table
    return parts


def flat_index():
    place = CORE * lax.axis_index("c")
    for axis in PLACES:
        place = place + STRIDE[axis] * lax.axis_index(axis)
    return place


def fom_kernel(target, forward, mode, sent, line, sem):
    rows = forward.at[0, :, pl.ds(ROWS // 2, TILE), :]
    copy = pltpu.make_async_copy(rows, line, sem)
    copy.start()
    copy.wait()
    re, im = line[0, 0:1, :], line[1, 0:1, :]
    mode_re, mode_im = mode[0:1, :], mode[1:2, :]
    over_re = jnp.sum(re * mode_re - im * mode_im, axis=1, keepdims=True)
    over_im = jnp.sum(re * mode_im + im * mode_re, axis=1, keepdims=True)
    fom = (over_re * over_re + over_im * over_im) / COLS
    lane = lax.broadcasted_iota(jnp.int32, (1, LANES), 1)
    row = jnp.where(lane < LANES // 2, fom, target[0])
    sent[...] = jnp.broadcast_to(row[None], sent.shape)


def field_kernel(away, tile_of, wl_index, forward, adjoint, out, fwd, adj, sems):
    core = lax.axis_index("c")
    keeper = (1 - core) if away else core
    parts = owner_parts(keeper)

    def owner(block):
        k, j = divmod(block, CUBE)
        total = CORE * keeper
        for shift, axis in zip((2, 1, 0), PLACES):
            total = total + parts[axis][((k >> shift) & 1) * 2 + ((j >> shift) & 1)]
        return total

    for block in range(HALF):
        row = pl.multiple_of(tile_of[owner(block)] * TILE, TILE)
        sem = sems.at[block // CHUNK]
        pltpu.make_async_copy(
            forward.at[0, :, pl.ds(row, TILE), :], fwd.at[block], sem
        ).start()
        pltpu.make_async_copy(
            adjoint.at[0, :, pl.ds(row, TILE), :], adj.at[block], sem
        ).start()
    freq = 1.0 + wl_index[0].astype(jnp.float32) / DEVICES
    square = freq * freq
    for chunk in range(HALF // CHUNK):
        these = pl.ds(chunk * CHUNK, CHUNK)
        for buffer in (fwd, adj):
            part = buffer.at[these]
            pltpu.make_async_copy(part, part, sems.at[chunk]).wait()
        for block in range(chunk * CHUNK, (chunk + 1) * CHUNK):
            out[block] = square * (
                fwd[block, 0] * adj[block, 0] - fwd[block, 1] * adj[block, 1]
            )


def weigh_kernel(foms, mine, other, out):
    me = flat_index()
    partner = me + CORE * (1 - 2 * lax.axis_index("c"))
    fom_sum = jnp.sum(foms[...], axis=0)[:, 0:1]
    scale = fom_sum / DEVICES + 1.0

    def weight(device):
        row = foms[device]
        return row[:, LANES // 2 : LANES // 2 + 1] - row[:, 0:1] / scale

    own, theirs = weight(me), weight(partner)
    for block in range(HALF):
        out[block] = own * mine[block] + theirs * other[block]


def shape_kernel(arrived, density, shaped, sent):
    total = arrived[0]
    for member in range(1, CUBE):
        total = total + arrived[member]
    bend = jnp.tanh(4.0 * (density[...] - 0.5))
    result = total * (4.0 * (1.0 - bend * bend))
    shaped[...] = result
    square = jnp.sum(result * result, axis=(0, 1), keepdims=True)
    sent[...] = jnp.broadcast_to(square[None], sent.shape)


def scale_kernel(squares, shaped, out):
    total = jnp.sum(squares[...], axis=0)[:, 0:1]
    norm = jnp.sqrt(total / (ROWS * COLS) + 1e-06)
    out[...] = shaped[...] / norm


def vmem():
    return pl.BlockSpec(memory_space=pltpu.VMEM)


def smem():
    return pl.BlockSpec(memory_space=pltpu.SMEM)


def hbm():
    return pl.BlockSpec(memory_space=pltpu.HBM)


def f32(*shape):
    return jax.ShapeDtypeStruct(shape, jnp.float32)


def grant(mib):
    return pltpu.CompilerParams(vmem_limit_bytes=mib * MIB)


def field(away, tile_of, wl_index, forward, adjoint):
    return pl.pallas_call(
        functools.partial(field_kernel, away),
        out_shape=f32(HALF, TILE, COLS),
        in_specs=[smem(), smem(), hbm(), hbm()],
        out_specs=vmem(),
        scratch_shapes=[
            pltpu.VMEM((HALF, 2, TILE, COLS), jnp.float32),
            pltpu.VMEM((HALF, 2, TILE, COLS), jnp.float32),
            pltpu.SemaphoreType.DMA((HALF // CHUNK,)),
        ],
        compiler_params=grant(16),
        name="field_away" if away else "field_own",
    )(tile_of, wl_index, forward, adjoint)


def exchanged(blocks, groups=None):
    return lax.all_to_all(blocks, AXES, 0, 0, tiled=True, axis_index_groups=groups)


def per_device(forward, adjoint, mode, target, wl_index, tile_of, density):
    fom_sent = pl.pallas_call(
        fom_kernel,
        out_shape=f32(DEVICES, 1, LANES),
        in_specs=[smem(), hbm(), vmem()],
        out_specs=vmem(),
        scratch_shapes=[
            pltpu.VMEM((2, TILE, COLS), jnp.float32),
            pltpu.SemaphoreType.DMA,
        ],
        compiler_params=grant(4),
        name="fom",
    )(target, forward, mode)
    foms = exchanged(fom_sent)
    away = field(True, tile_of, wl_index, forward, adjoint)
    other = lax.ppermute(away, "c", [(0, 1), (1, 0)])
    mine = field(False, tile_of, wl_index, forward, adjoint)
    weighted = pl.pallas_call(
        weigh_kernel,
        out_shape=f32(HALF, TILE, COLS),
        in_specs=[vmem(), vmem(), vmem()],
        out_specs=vmem(),
        compiler_params=grant(8),
        name="weigh",
    )(foms, mine, other)
    nearer = exchanged(weighted.reshape(CUBE, CUBE * TILE, COLS), cubes(FIRST)).sum(0)
    arrived = exchanged(nearer.reshape(CUBE, TILE, COLS), cubes(SECOND))
    shaped, square_sent = pl.pallas_call(
        shape_kernel,
        out_shape=[f32(TILE, COLS), f32(DEVICES, 1, LANES)],
        in_specs=[vmem(), vmem()],
        out_specs=[vmem(), vmem()],
        compiler_params=grant(4),
        name="shape",
    )(arrived, density)
    squares = exchanged(square_sent)
    return pl.pallas_call(
        scale_kernel,
        out_shape=f32(TILE, COLS),
        in_specs=[vmem(), vmem()],
        out_specs=vmem(),
        compiler_params=grant(4),
        name="scale",
    )(squares, shaped)


def solution(mesh):
    split = Mesh(mesh.devices.reshape(SIDE, SIDE, 2, SIDE), AXES)
    rows = P(AXES, None)
    placed = (
        P(AXES, None, None, None),
        P(AXES, None, None, None),
        P(),
        P(AXES),
        P(AXES),
        P(),
        rows,
    )
    return jax.shard_map(
        per_device, mesh=split, in_specs=placed, out_specs=rows, check_vma=False
    )
```

time: 143 us -> 97.6 us (0.68)
  blocking collectives: 85.5 us -> 50.7 us
  Pallas kernels: 0 us -> 19 us
  other arithmetic: 16.5 us -> 0.14 us
  waiting for transfers between devices: 8.85 us -> 0.01 us
  between operations: 5.43 us -> 1.42 us
  local copies, waits for them, and re-layouts: 12.2 us -> 14.2 us
  starting transfers between devices: 13.6 us -> 11.7 us
    all_to_all x4 -> x3, blocking collectives: 85.5 us -> 50.7 us  [exchanged(): lax.all_to_all(blocks, AXES, 0, 0, tiled=True, axis_index_groups=groups)]
    pallas_call x0 -> x6, Pallas kernels: none -> 19 us  [the longest x2 15.1 us: field(): pl.pallas_call(functools.partial(field_kernel, away), out_shape=f32(HALF,...]
    unnamed x2 -> x16, local copies, waits for them, and re-layouts: 0.01 us -> 14.2 us
    all_to_all x2 -> x1, waiting for transfers between devices: 8.85 us -> 0.01 us  [exchanged(): lax.all_to_all(blocks, AXES, 0, 0, tiled=True, axis_index_groups=groups)]
    mul x1 -> x0, other arithmetic: 8.75 us -> none  [per_device(): weight * field]
    reduce_sum x8 -> x1, other arithmetic: 6.48 us -> 0.14 us  [per_device(): exchanged(weighted.reshape(CUBE, CUBE * TILE, COLS), cubes(FIRST)).sum(0)]
    gather x1 -> x0, local copies, waits for them, and re-layouts: 4.97 us -> none  [per_device(): (weight * field).reshape(devices, tile_rows, cols)[tile_of]]
    all_to_all x2 -> x1, starting transfers between devices: 13.6 us -> 10.2 us  [exchanged(): lax.all_to_all(blocks, AXES, 0, 0, tiled=True, axis_index_groups=groups)]
  transfers between devices with their start and end apart: 2 -> 2, of which waited for: 2 -> 0; matrix products, arithmetic and copies ran while one was open for 0% -> 0% of each run, Pallas kernels for 0% -> 8%
where the time goes in v1:
time: 97.6 us; the launch traced here: 97.1 us
  blocking collectives  50.7 us (52%)
  Pallas kernels  19 us (19%)
  local copies, waits for them, and re-layouts  14.2 us (15%)
  starting transfers between devices  11.7 us (12%)
  between operations  1.42 us (1%)
    all_to_all x3, blocking collectives, exchanged(): lax.all_to_all(blocks, AXES, 0, 0, tiled=True, axis_index_groups=groups)  50.7 us
    pallas_call x2, Pallas kernels, field(): pl.pallas_call(functools.partial(field_kernel, away), out_shape=f32(HALF,...  15.1 us
    unnamed x16, local copies, waits for them, and re-layouts  14.2 us
    all_to_all x1, starting transfers between devices, exchanged(): lax.all_to_all(blocks, AXES, 0, 0, tiled=True, axis_index_groups=groups)  10.2 us
    pallas_call x1, Pallas kernels, per_device(): pl.pallas_call(weigh_kernel, out_shape=f32(HALF, TILE, COLS), in_specs=[v...  2.11 us
  transfers between devices with their start and end apart: 2, of which 0 were waited for; matrix products, arithmetic and copies ran while one was open for 0% of the time, Pallas kernels for 8%

profile of v1, /device:TPU:1, one launch (start us, length us, event | category | flops | bytes accessed | tf_op | source)
XLA Modules:
  0.0 97.1 jit_solution(6058258354495270202)
XLA Ops:
  0.7 0.0 copy-start
  0.7 3.4 %copy-done = f32[1,2,1024,1024]{3,2,1,0:T(8,128)S(1)} copy-done((f32[1,2,1024,1024]{3,2,1,0:T(8,128)S(1)}, f32[1,2,1024,1024]{3,2,1,0:T(8,128)}, u32[]{:S(2)}) %copy-start) | copy-done | bytes 8388632
  4.0 3.4 %copy-done.2 = f32[1,2,1024,1024]{3,2,1,0:T(8,128)S(1)} copy-done((f32[1,2,1024,1024]{3,2,1,0:T(8,128)S(1)}, f32[1,2,1024,1024]{3,2,1,0:T(8,128)}, u32[]{:S(2)}) %copy-start.2) | copy-done | bytes 8388632
  7.4 0.7 copy-done.6
  8.1 8.2 %field_away.1 = f32[64,8,1024]{2,1,0:T(8,128)} custom-call(s32[128]{0:T(128)S(1)} %copy-done.6, s32[1]{0:T(128)S(6)} %copy.9.wl_index, f32[1,2,1024,1024]{3,2,1,0:T(8,128)S(1)} %copy-done, f32[1,2,1024,1024]{3,2,1,0:T(8,128)S(1)} %copy-done.2), custom_call_target="tpu_custom_call" | custom-call | tf_op jit(solution)/shard_map/field_away/pallas_call | solution.py:180
  16.3 1.5 %collective-permute-start = (f32[64,8,1024]{2,1,0:T(8,128)}, f32[64,8,1024]{2,1,0:T(8,128)}, u32[]{:S(2)}, u32[]{:S(2)}) collective-permute-start(f32[64,8,1024]{2,1,0:T(8,128)} %field_away.1), channel_id=1, source_target_pairs={{0,4},{4,0},{1,5},{5,1},{2,6},{6,2},{3,7},{7,3},{8,12},{12,8},{9,1... | collective-permute-start | bytes 6291464 | tf_op jit(solution)/shard_map/ppermute | solution.py:214
  18.5 0.0 copy-done.5
  18.5 0.0 copy-start.7
  18.5 0.8 fom.1
  19.3 10.2 %all-to-all-start = ((f32[128,1,128]{2,1,0:T(1,128)}), f32[128,1,128]{2,1,0:T(1,128)S(1)}, u32[]{:S(2)}, u32[]{:S(2)}) async-start(f32[128,1,128]{2,1,0:T(1,128)} %fom.1), calls=%async_computation | async-start | bytes 131072 | tf_op jit(solution)/shard_map/all_to_all | solution.py:196
  29.5 0.0 copy-start.1
  29.5 3.4 %copy-done.1 = f32[1,2,1024,1024]{3,2,1,0:T(8,128)S(1)} copy-done((f32[1,2,1024,1024]{3,2,1,0:T(8,128)S(1)}, f32[1,2,1024,1024]{3,2,1,0:T(8,128)}, u32[]{:S(2)}) %copy-start.1) | copy-done | bytes 8388632
  32.9 3.4 %copy-done.3 = f32[1,2,1024,1024]{3,2,1,0:T(8,128)S(1)} copy-done((f32[1,2,1024,1024]{3,2,1,0:T(8,128)S(1)}, f32[1,2,1024,1024]{3,2,1,0:T(8,128)}, u32[]{:S(2)}) %copy-start.3) | copy-done | bytes 8388632
  36.3 6.9 %field_own.1.mine = f32[64,8,1024]{2,1,0:T(8,128)S(1)} custom-call(s32[128]{0:T(128)S(1)} %copy-done.7, s32[1]{0:T(128)S(6)} %copy.9.wl_index, f32[1,2,1024,1024]{3,2,1,0:T(8,128)S(1)} %copy-done.1, f32[1,2,1024,1024]{3,2,1,0:T(8,128)S(1)} %copy-done.3), custom_call_target="tpu_custom_call" | custom-call | tf_op jit(solution)/shard_map/field_own/pallas_call | solution.py:180
  43.1 0.0 all-to-all-done.foms
  43.2 0.0 collective-permute-done.other
  43.2 2.1 %weigh.1 = f32[64,8,1024]{2,1,0:T(8,128)S(1)} custom-call(f32[128,1,128]{2,1,0:T(1,128)S(1)} %all-to-all-done.foms, f32[64,8,1024]{2,1,0:T(8,128)S(1)} %field_own.1.mine, f32[64,8,1024]{2,1,0:T(8,128)} %collective-permute-done.other), custom_call_target="tpu_custom_call" | custom-call | tf_op jit(solution)/shard_map/weigh/pallas_call | solution.py:216
  45.3 27.7 %all_to_all.20 = f32[8,64,1024]{2,1,0:T(8,128)S(1)} all-to-all(f32[8,64,1024]{2,1,0:T(8,128)S(1)} %bitcast.2), channel_id=1, replica_groups={{0,1,8,9,32,33,40,41},{2,3,10,11,34,35,42,43},{16,17,24,25,48,49,56,57}..., dimensions={0} | all-to-all | bytes 4194304 | tf_op jit(solution)/shard_map/all_to_all | solution.py:196
  73.0 0.1 reduce_sum.9
  73.2 7.9 %all_to_all.21.arrived = f32[8,8,1024]{2,1,0:T(8,128)S(1)} all-to-all(f32[8,8,1024]{2,1,0:T(8,128)S(1)} %bitcast.3), channel_id=1, replica_groups={{0,3,24,27,96,99,120,123},{1,2,25,26,97,98,121,122},{8,11,16,19,104,107..., dimensions={0} | all-to-all | bytes 524288 | tf_op jit(solution)/shard_map/all_to_all | solution.py:196
  81.0 0.0 copy-done.4
  81.0 0.2 shape.1
  81.2 15.1 %all_to_all.22.squares = f32[128,1,128]{2,1,0:T(1,128)S(1)} all-to-all(f32[128,1,128]{2,1,0:T(1,128)S(1)} %get-tuple-element.7), channel_id=1, replica_groups=mesh['x'=4,'y'=4,'c'=2,'z'=4] {'x','y','c','z'}, dimensions={0} | all-to-all | bytes 131072 | tf_op jit(solution)/shard_map/all_to_all | solution.py:196
  96.3 0.8 scale.1
  (6 shorter events, 0.0 us)
Async XLA Ops:
  0.7 3.4 %copy-start = (f32[1,2,1024,1024]{3,2,1,0:T(8,128)S(1)}, f32[1,2,1024,1024]{3,2,1,0:T(8,128)}, u32[]{:S(2)}) copy-start(f32[1,2,1024,1024]{3,2,1,0:T(8,128)} %forward.5) | copy-start | bytes 25165828
  4.0 3.4 %copy-start.2 = (f32[1,2,1024,1024]{3,2,1,0:T(8,128)S(1)}, f32[1,2,1024,1024]{3,2,1,0:T(8,128)}, u32[]{:S(2)}) copy-start(f32[1,2,1024,1024]{3,2,1,0:T(8,128)} %adjoint.3) | copy-start | bytes 25165828
  7.4 0.7 copy-start.6
  8.1 10.4 %copy-start.5 = (f32[2,1024]{1,0:T(2,128)S(1)}, f32[2,1024]{1,0:T(2,128)}, u32[]{:S(2)}) copy-start(f32[2,1024]{1,0:T(2,128)} %mode.1) | copy-start | bytes 24580
  16.3 26.9 %collective-permute-start = (f32[64,8,1024]{2,1,0:T(8,128)}, f32[64,8,1024]{2,1,0:T(8,128)}, u32[]{:S(2)}, u32[]{:S(2)}) collective-permute-start(f32[64,8,1024]{2,1,0:T(8,128)} %field_away.1), channel_id=1, source_target_pairs={{0,4},{4,0},{1,5},{5,1},{2,6},{6,2},{3,7},{7,3},{8,12},{12,8},{9,1... | collective-permute-start | bytes 6291464 | tf_op jit(solution)/shard_map/ppermute | solution.py:214
  18.5 11.0 %copy-start.7 = (s32[128]{0:T(128)S(1)}, s32[128]{0:T(128)}, u32[]{:S(2)}) copy-start(s32[128]{0:T(128)} %tile_of.3) | copy-start | bytes 1540
  19.3 23.9 %all-to-all-start = ((f32[128,1,128]{2,1,0:T(1,128)}), f32[128,1,128]{2,1,0:T(1,128)S(1)}, u32[]{:S(2)}, u32[]{:S(2)}) async-start(f32[128,1,128]{2,1,0:T(1,128)} %fom.1), calls=%async_computation | async-start | bytes 131072 | tf_op jit(solution)/shard_map/all_to_all | solution.py:196
  29.5 3.4 %copy-start.1 = (f32[1,2,1024,1024]{3,2,1,0:T(8,128)S(1)}, f32[1,2,1024,1024]{3,2,1,0:T(8,128)}, u32[]{:S(2)}) copy-start(f32[1,2,1024,1024]{3,2,1,0:T(8,128)} %forward.5) | copy-start | bytes 25165828
  32.9 3.4 %copy-start.3 = (f32[1,2,1024,1024]{3,2,1,0:T(8,128)S(1)}, f32[1,2,1024,1024]{3,2,1,0:T(8,128)}, u32[]{:S(2)}) copy-start(f32[1,2,1024,1024]{3,2,1,0:T(8,128)} %adjoint.3) | copy-start | bytes 25165828
  73.0 8.0 %copy-start.4 = (f32[8,1024]{1,0:T(8,128)S(1)}, f32[8,1024]{1,0:T(8,128)}, u32[]{:S(2)}) copy-start(f32[8,1024]{1,0:T(8,128)} %density.1) | copy-start | bytes 98308

commit v2 on v1

--- a/solution.py
+++ b/solution.py
@@ -1,5 +1,3 @@
-import functools
-
 import jax
 import jax.numpy as jnp
 from jax import lax
@@ -22,6 +20,7 @@
 CHUNK = 8
 LANES = 128
 MIB = 1 << 20
+FIELD_MIB = 20
 
 EVEN = ((0, 1), (2, 3))
 ODD = ((0, 3), (1, 2))
@@ -75,42 +74,22 @@
     return place
 
 
-def fom_kernel(target, forward, mode, sent, line, sem):
-    rows = forward.at[0, :, pl.ds(ROWS // 2, TILE), :]
-    copy = pltpu.make_async_copy(rows, line, sem)
-    copy.start()
-    copy.wait()
-    re, im = line[0, 0:1, :], line[1, 0:1, :]
-    mode_re, mode_im = mode[0:1, :], mode[1:2, :]
-    over_re = jnp.sum(re * mode_re - im * mode_im, axis=1, keepdims=True)
-    over_im = jnp.sum(re * mode_im + im * mode_re, axis=1, keepdims=True)
-    fom = (over_re * over_re + over_im * over_im) / COLS
-    lane = lax.broadcasted_iota(jnp.int32, (1, LANES), 1)
-    row = jnp.where(lane < LANES // 2, fom, target[0])
-    sent[...] = jnp.broadcast_to(row[None], sent.shape)
-
-
-def field_kernel(away, tile_of, wl_index, forward, adjoint, out, fwd, adj, sems):
+def gather_fields(away, tile_of, wl_index, forward, adjoint, out, fwd, adj, sems, between):
     core = lax.axis_index("c")
     keeper = (1 - core) if away else core
     parts = owner_parts(keeper)
-
-    def owner(block):
+    for block in range(HALF):
         k, j = divmod(block, CUBE)
-        total = CORE * keeper
+        owner = CORE * keeper
         for shift, axis in zip((2, 1, 0), PLACES):
-            total = total + parts[axis][((k >> shift) & 1) * 2 + ((j >> shift) & 1)]
-        return total
-
-    for block in range(HALF):
-        row = pl.multiple_of(tile_of[owner(block)] * TILE, TILE)
+            bits = ((k >> shift) & 1) * 2 + ((j >> shift) & 1)
+            owner = owner + parts[axis][bits]
+        row = pl.multiple_of(tile_of[owner] * TILE, TILE)
         sem = sems.at[block // CHUNK]
-        pltpu.make_async_copy(
-            forward.at[0, :, pl.ds(row, TILE), :], fwd.at[block], sem
-        ).start()
-        pltpu.make_async_copy(
-            adjoint.at[0, :, pl.ds(row, TILE), :], adj.at[block], sem
-        ).start()
+        for source, buffer in ((forward, fwd), (adjoint, adj)):
+            tile = source.at[0, :, pl.ds(row, TILE), :]
+            pltpu.make_async_copy(tile, buffer.at[block], sem).start()
+    between()
     freq = 1.0 + wl_index[0].astype(jnp.float32) / DEVICES
     square = freq * freq
     for chunk in range(HALF // CHUNK):
@@ -124,7 +103,65 @@
             )
 
 
-def weigh_kernel(foms, mine, other, out):
+def away_kernel(
+    tile_of,
+    forward,
+    adjoint,
+    mode,
+    wl_index_in,
+    target_in,
+    sent,
+    out,
+    fwd,
+    adj,
+    sems,
+    line,
+    wl_index,
+    target,
+    line_sem,
+    scalar_sems,
+):
+    rows = forward.at[0, :, pl.ds(ROWS // 2, TILE), :]
+    line_copy = pltpu.make_async_copy(rows, line, line_sem)
+    wl_copy = pltpu.make_async_copy(wl_index_in, wl_index, scalar_sems.at[0])
+    target_copy = pltpu.make_async_copy(target_in, target, scalar_sems.at[1])
+    for copy in (line_copy, wl_copy, target_copy):
+        copy.start()
+
+    def send_fom():
+        for copy in (line_copy, wl_copy, target_copy):
+            copy.wait()
+        re, im = line[0, 0:1, :], line[1, 0:1, :]
+        mode_re, mode_im = mode[0:1, :], mode[1:2, :]
+        over_re = jnp.sum(re * mode_re - im * mode_im, axis=1, keepdims=True)
+        over_im = jnp.sum(re * mode_im + im * mode_re, axis=1, keepdims=True)
+        fom = (over_re * over_re + over_im * over_im) / COLS
+        lane = lax.broadcasted_iota(jnp.int32, (1, LANES), 1)
+        row = jnp.where(lane < LANES // 2, fom, target[0])
+        sent[...] = jnp.broadcast_to(row[None], sent.shape)
+
+    gather_fields(
+        True, tile_of, wl_index, forward, adjoint, out, fwd, adj, sems, send_fom
+    )
+
+
+def own_kernel(
+    tile_of, forward, adjoint, wl_index_in, after, out, fwd, adj, sems, wl_index, sem
+):
+    wl_copy = pltpu.make_async_copy(wl_index_in, wl_index, sem)
+    wl_copy.start()
+    gather_fields(
+        False, tile_of, wl_index, forward, adjoint, out, fwd, adj, sems, wl_copy.wait
+    )
+
+
+def weigh_kernel(foms, mine, other_hbm, out, other, sems):
+    copies = []
+    for chunk in range(HALF // CHUNK):
+        these = pl.ds(chunk * CHUNK, CHUNK)
+        copy = pltpu.make_async_copy(other_hbm.at[these], other.at[these], sems.at[chunk])
+        copy.start()
+        copies.append(copy)
     me = flat_index()
     partner = me + CORE * (1 - 2 * lax.axis_index("c"))
     fom_sum = jnp.sum(foms[...], axis=0)[:, 0:1]
@@ -136,6 +173,8 @@
 
     own, theirs = weight(me), weight(partner)
     for block in range(HALF):
+        if block % CHUNK == 0:
+            copies[block // CHUNK].wait()
         out[block] = own * mine[block] + theirs * other[block]
 
 
@@ -172,55 +211,71 @@
     return jax.ShapeDtypeStruct(shape, jnp.float32)
 
 
+def vmem_f32(*shape):
+    return pltpu.VMEM(shape, jnp.float32)
+
+
+def in_hbm(array):
+    return pltpu.with_memory_space_constraint(array, pltpu.HBM)
+
+
 def grant(mib):
     return pltpu.CompilerParams(vmem_limit_bytes=mib * MIB)
 
 
-def field(away, tile_of, wl_index, forward, adjoint):
-    return pl.pallas_call(
-        functools.partial(field_kernel, away),
-        out_shape=f32(HALF, TILE, COLS),
-        in_specs=[smem(), smem(), hbm(), hbm()],
+def exchanged(blocks, groups=None):
+    return lax.all_to_all(blocks, AXES, 0, 0, tiled=True, axis_index_groups=groups)
+
+
+def per_device(forward, adjoint, mode, target, wl_index, tile_of, density):
+    forward, adjoint, mode, tile_of = (
+        in_hbm(array) for array in (forward, adjoint, mode, tile_of)
+    )
+    buffer = pltpu.VMEM((HALF, 2, TILE, COLS), jnp.float32)
+    gather_scratch = [buffer, buffer, pltpu.SemaphoreType.DMA((HALF // CHUNK,))]
+    fom_sent, away = pl.pallas_call(
+        away_kernel,
+        out_shape=[vmem_f32(DEVICES, 1, LANES), vmem_f32(HALF, TILE, COLS)],
+        in_specs=[smem(), hbm(), hbm(), vmem(), hbm(), hbm()],
+        out_specs=[vmem(), vmem()],
+        scratch_shapes=[
+            *gather_scratch,
+            pltpu.VMEM((2, TILE, COLS), jnp.float32),
+            pltpu.SMEM((1,), jnp.int32),
+            pltpu.SMEM((1,), jnp.float32),
+            pltpu.SemaphoreType.DMA,
+            pltpu.SemaphoreType.DMA((2,)),
+        ],
+        compiler_params=grant(FIELD_MIB),
+        name="field_away",
+    )(tile_of, forward, adjoint, mode, wl_index, target)
+    other = lax.ppermute(away, "c", [(0, 1), (1, 0)])
+    foms = exchanged(fom_sent)
+    mine = pl.pallas_call(
+        own_kernel,
+        out_shape=vmem_f32(HALF, TILE, COLS),
+        in_specs=[smem(), hbm(), hbm(), hbm(), hbm()],
         out_specs=vmem(),
         scratch_shapes=[
-            pltpu.VMEM((HALF, 2, TILE, COLS), jnp.float32),
-            pltpu.VMEM((HALF, 2, TILE, COLS), jnp.float32),
+            *gather_scratch,
+            pltpu.SMEM((1,), jnp.int32),
+            pltpu.SemaphoreType.DMA,
+        ],
+        compiler_params=grant(FIELD_MIB),
+        name="field_own",
+    )(tile_of, forward, adjoint, wl_index, fom_sent)
+    weighted = pl.pallas_call(
+        weigh_kernel,
+        out_shape=vmem_f32(HALF, TILE, COLS),
+        in_specs=[vmem(), vmem(), hbm()],
+        out_specs=vmem(),
+        scratch_shapes=[
+            pltpu.VMEM((HALF, TILE, COLS), jnp.float32),
             pltpu.SemaphoreType.DMA((HALF // CHUNK,)),
         ],
-        compiler_params=grant(16),
-        name="field_away" if away else "field_own",
-    )(tile_of, wl_index, forward, adjoint)
-
-
-def exchanged(blocks, groups=None):
-    return lax.all_to_all(blocks, AXES, 0, 0, tiled=True, axis_index_groups=groups)
-
-
-def per_device(forward, adjoint, mode, target, wl_index, tile_of, density):
-    fom_sent = pl.pallas_call(
-        fom_kernel,
-        out_shape=f32(DEVICES, 1, LANES),
-        in_specs=[smem(), hbm(), vmem()],
-        out_specs=vmem(),
-        scratch_shapes=[
-            pltpu.VMEM((2, TILE, COLS), jnp.float32),
-            pltpu.SemaphoreType.DMA,
-        ],
-        compiler_params=grant(4),
-        name="fom",
-    )(target, forward, mode)
-    foms = exchanged(fom_sent)
-    away = field(True, tile_of, wl_index, forward, adjoint)
-    other = lax.ppermute(away, "c", [(0, 1), (1, 0)])
-    mine = field(False, tile_of, wl_index, forward, adjoint)
-    weighted = pl.pallas_call(
-        weigh_kernel,
-        out_shape=f32(HALF, TILE, COLS),
-        in_specs=[vmem(), vmem(), vmem()],
-        out_specs=vmem(),
         compiler_params=grant(8),
         name="weigh",
-    )(foms, mine, other)
+    )(foms, mine, in_hbm(other))
     nearer = exchanged(weighted.reshape(CUBE, CUBE * TILE, COLS), cubes(FIRST)).sum(0)
     arrived = exchanged(nearer.reshape(CUBE, TILE, COLS), cubes(SECOND))
     shaped, square_sent = pl.pallas_call(

time: 97.6 us -> 77.5 us (0.79)
  local copies, waits for them, and re-layouts: 14.2 us -> 0.01 us
  Pallas kernels: 19 us -> 13.2 us
  blocking collectives: 50.7 us -> 45.4 us
  waiting for transfers between devices: 0.01 us -> 5.31 us
    unnamed x16 -> x2, local copies, waits for them, and re-layouts: 14.2 us -> 0.01 us
    pallas_call x4 -> x3, Pallas kernels: 18 us -> 12.2 us  [the longest x1 6.25 us: per_device(): pl.pallas_call(away_kernel, out_shape=[vmem_f32(DEVICES, 1, LANES), vmem_...]
    all_to_all x1, waiting for transfers between devices: 0.01 us -> 5.31 us  [exchanged(): lax.all_to_all(blocks, AXES, 0, 0, tiled=True, axis_index_groups=groups)]
    all_to_all x3, blocking collectives: 50.7 us -> 45.4 us  [exchanged(): lax.all_to_all(blocks, AXES, 0, 0, tiled=True, axis_index_groups=groups)]
  transfers between devices with their start and end apart: 2 -> 2, of which waited for: 0 -> 1; matrix products, arithmetic and copies ran while one was open for 0% -> 0% of each run, Pallas kernels for 8% -> 6%
where the time goes in v2:
time: 77.5 us; the launch traced here: 77.1 us
  blocking collectives  45.4 us (59%)
  Pallas kernels  13.2 us (17%)
  starting transfers between devices  11.7 us (15%)
  waiting for transfers between devices  5.31 us (7%)
  between operations  1.35 us (2%)
    all_to_all x3, blocking collectives, exchanged(): lax.all_to_all(blocks, AXES, 0, 0, tiled=True, axis_index_groups=groups)  45.4 us
    all_to_all x1, starting transfers between devices, exchanged(): lax.all_to_all(blocks, AXES, 0, 0, tiled=True, axis_index_groups=groups)  10.2 us
    pallas_call x1, Pallas kernels, per_device(): pl.pallas_call(away_kernel, out_shape=[vmem_f32(DEVICES, 1, LANES), vmem_...  6.25 us
    all_to_all x1, waiting for transfers between devices, exchanged(): lax.all_to_all(blocks, AXES, 0, 0, tiled=True, axis_index_groups=groups)  5.31 us
    pallas_call x1, Pallas kernels, per_device(): pl.pallas_call(own_kernel, out_shape=vmem_f32(HALF, TILE, COLS), in_specs...  4.36 us
    pallas_call x1, Pallas kernels, per_device(): pl.pallas_call(weigh_kernel, out_shape=vmem_f32(HALF, TILE, COLS), in_spe...  1.64 us
  transfers between devices with their start and end apart: 2, of which 1 were waited for; matrix products, arithmetic and copies ran while one was open for 0% of the time, Pallas kernels for 6%

profile of v2, /device:TPU:1, one launch (start us, length us, event | category | flops | bytes accessed | tf_op | source)
XLA Modules:
  0.0 77.1 jit_solution(11868961737943120515)
XLA Ops:
  1.3 6.3 %field_away.1 = (f32[128,1,128]{2,1,0:T(1,128)}, f32[64,8,1024]{2,1,0:T(8,128)}) custom-call(s32[128]{0:T(128)} %tile_of.3, f32[1,2,1024,1024]{3,2,1,0:T(8,128)} %forward.3, f32[1,2,1024,1024]{3,2,1,0:T(8,128)} %adjoint.3, f32[2,1024]{1,0:T(2,128)} %mode.1, s32[1]{0:T(128)S(6)} %copy.9.wl_index_in, f32[1]{0:T(128)S(6)} %copy.8.target_in), custom_call_target="tpu_custom_call" | custom-call | tf_op jit(solution)/shard_map/field_away/pallas_call | solution.py:236
  7.6 1.5 %collective-permute-start = (f32[64,8,1024]{2,1,0:T(8,128)}, f32[64,8,1024]{2,1,0:T(8,128)}, u32[]{:S(2)}, u32[]{:S(2)}) collective-permute-start(f32[64,8,1024]{2,1,0:T(8,128)} %get-tuple-element.10), channel_id=1, source_target_pairs={{0,4},{4,0},{1,5},{5,1},{2,6},{6,2},{3,7},{7,3},{8,12},{12,8},{9,1... | collective-permute-start | bytes 6291464 | tf_op jit(solution)/shard_map/ppermute | solution.py:252
  9.1 10.2 %all-to-all-start = ((f32[128,1,128]{2,1,0:T(1,128)}), f32[128,1,128]{2,1,0:T(1,128)S(1)}, u32[]{:S(2)}, u32[]{:S(2)}) async-start(f32[128,1,128]{2,1,0:T(1,128)} %get-tuple-element.9.after), calls=%async_computation | async-start | bytes 131072 | tf_op jit(solution)/shard_map/all_to_all | solution.py:227
  19.3 4.4 %field_own.1.mine = f32[64,8,1024]{2,1,0:T(8,128)S(1)} custom-call(s32[128]{0:T(128)} %tile_of.3, f32[1,2,1024,1024]{3,2,1,0:T(8,128)} %forward.3, f32[1,2,1024,1024]{3,2,1,0:T(8,128)} %adjoint.3, s32[1]{0:T(128)S(6)} %copy.9.wl_index_in, f32[128,1,128]{2,1,0:T(1,128)} %get-tuple-element.9.after), custom_call_target="tpu_custom_call" | custom-call | tf_op jit(solution)/shard_map/field_own/pallas_call | solution.py:254
  23.6 5.3 %all-to-all-done.foms = f32[128,1,128]{2,1,0:T(1,128)S(1)} async-done(((f32[128,1,128]{2,1,0:T(1,128)}), f32[128,1,128]{2,1,0:T(1,128)S(1)}, u32[]{:S(2)}, u32[]{:S(2)}) %all-to-all-start) | async-done | bytes 65568 | tf_op jit(solution)/shard_map/all_to_all | solution.py:227
  28.9 0.0 collective-permute-done.other_hbm
  28.9 1.6 %weigh.1 = f32[64,8,1024]{2,1,0:T(8,128)S(1)} custom-call(f32[128,1,128]{2,1,0:T(1,128)S(1)} %all-to-all-done.foms, f32[64,8,1024]{2,1,0:T(8,128)S(1)} %field_own.1.mine, f32[64,8,1024]{2,1,0:T(8,128)} %collective-permute-done.other_hbm), custom_call_target="tpu_custom_call" | custom-call | tf_op jit(solution)/shard_map/weigh/pallas_call | solution.py:267
  30.6 22.4 %all_to_all.20 = f32[8,64,1024]{2,1,0:T(8,128)S(1)} all-to-all(f32[8,64,1024]{2,1,0:T(8,128)S(1)} %bitcast.2), channel_id=1, replica_groups={{0,1,8,9,32,33,40,41},{2,3,10,11,34,35,42,43},{16,17,24,25,48,49,56,57}..., dimensions={0} | all-to-all | bytes 4194304 | tf_op jit(solution)/shard_map/all_to_all | solution.py:227
  53.0 0.0 copy-start
  53.0 0.1 reduce_sum.9
  53.2 7.9 %all_to_all.21.arrived = f32[8,8,1024]{2,1,0:T(8,128)S(1)} all-to-all(f32[8,8,1024]{2,1,0:T(8,128)S(1)} %bitcast.3), channel_id=1, replica_groups={{0,3,24,27,96,99,120,123},{1,2,25,26,97,98,121,122},{8,11,16,19,104,107..., dimensions={0} | all-to-all | bytes 524288 | tf_op jit(solution)/shard_map/all_to_all | solution.py:227
  61.1 0.0 copy-done
  61.1 0.2 shape.1
  61.2 15.1 %all_to_all.22.squares = f32[128,1,128]{2,1,0:T(1,128)S(1)} all-to-all(f32[128,1,128]{2,1,0:T(1,128)S(1)} %get-tuple-element.11), channel_id=1, replica_groups=mesh['x'=4,'y'=4,'c'=2,'z'=4] {'x','y','c','z'}, dimensions={0} | all-to-all | bytes 131072 | tf_op jit(solution)/shard_map/all_to_all | solution.py:227
  76.3 0.8 %scale.1 = f32[8,1024]{1,0:T(8,128)} custom-call(f32[128,1,128]{2,1,0:T(1,128)S(1)} %all_to_all.22.squares, f32[8,1024]{1,0:T(8,128)S(1)} %get-tuple-element.12.shaped), custom_call_target="tpu_custom_call" | custom-call | tf_op jit(solution)/shard_map/scale/pallas_call | solution.py:290
Async XLA Ops:
  7.6 21.4 %collective-permute-start = (f32[64,8,1024]{2,1,0:T(8,128)}, f32[64,8,1024]{2,1,0:T(8,128)}, u32[]{:S(2)}, u32[]{:S(2)}) collective-permute-start(f32[64,8,1024]{2,1,0:T(8,128)} %get-tuple-element.10), channel_id=1, source_target_pairs={{0,4},{4,0},{1,5},{5,1},{2,6},{6,2},{3,7},{7,3},{8,12},{12,8},{9,1... | collective-permute-start | bytes 6291464 | tf_op jit(solution)/shard_map/ppermute | solution.py:252
  9.1 19.9 %all-to-all-start = ((f32[128,1,128]{2,1,0:T(1,128)}), f32[128,1,128]{2,1,0:T(1,128)S(1)}, u32[]{:S(2)}, u32[]{:S(2)}) async-start(f32[128,1,128]{2,1,0:T(1,128)} %get-tuple-element.9.after), calls=%async_computation | async-start | bytes 131072 | tf_op jit(solution)/shard_map/all_to_all | solution.py:227
  53.0 8.0 %copy-start = (f32[8,1024]{1,0:T(8,128)S(1)}, f32[8,1024]{1,0:T(8,128)}, u32[]{:S(2)}) copy-start(f32[8,1024]{1,0:T(8,128)} %density.1) | copy-start | bytes 98308

commit v3 on v2

--- a/solution.py
+++ b/solution.py
@@ -17,7 +17,7 @@
 TILE = 8
 CUBE = 8
 HALF = DEVICES // 2
-CHUNK = 8
+CHUNK = 4
 LANES = 128
 MIB = 1 << 20
 FIELD_MIB = 20
@@ -107,29 +107,28 @@
     tile_of,
     forward,
     adjoint,
-    mode,
-    wl_index_in,
-    target_in,
+    mode_hbm,
+    wl_index,
+    target,
     sent,
     out,
     fwd,
     adj,
     sems,
     line,
-    wl_index,
-    target,
     line_sem,
-    scalar_sems,
+    mode,
+    mode_sem,
 ):
     rows = forward.at[0, :, pl.ds(ROWS // 2, TILE), :]
     line_copy = pltpu.make_async_copy(rows, line, line_sem)
-    wl_copy = pltpu.make_async_copy(wl_index_in, wl_index, scalar_sems.at[0])
-    target_copy = pltpu.make_async_copy(target_in, target, scalar_sems.at[1])
-    for copy in (line_copy, wl_copy, target_copy):
+    mode_copy = pltpu.make_async_copy(mode_hbm, mode, mode_sem)
+    small = (line_copy, mode_copy)
+    for copy in small:
         copy.start()
 
     def send_fom():
-        for copy in (line_copy, wl_copy, target_copy):
+        for copy in small:
             copy.wait()
         re, im = line[0, 0:1, :], line[1, 0:1, :]
         mode_re, mode_im = mode[0:1, :], mode[1:2, :]
@@ -146,12 +145,10 @@
 
 
 def own_kernel(
-    tile_of, forward, adjoint, wl_index_in, after, out, fwd, adj, sems, wl_index, sem
+    tile_of, forward, adjoint, wl_index, after, out, fwd, adj, sems
 ):
-    wl_copy = pltpu.make_async_copy(wl_index_in, wl_index, sem)
-    wl_copy.start()
     gather_fields(
-        False, tile_of, wl_index, forward, adjoint, out, fwd, adj, sems, wl_copy.wait
+        False, tile_of, wl_index, forward, adjoint, out, fwd, adj, sems, lambda: None
     )
 
 
@@ -236,15 +233,14 @@
     fom_sent, away = pl.pallas_call(
         away_kernel,
         out_shape=[vmem_f32(DEVICES, 1, LANES), vmem_f32(HALF, TILE, COLS)],
-        in_specs=[smem(), hbm(), hbm(), vmem(), hbm(), hbm()],
+        in_specs=[smem(), hbm(), hbm(), hbm(), smem(), smem()],
         out_specs=[vmem(), vmem()],
         scratch_shapes=[
             *gather_scratch,
             pltpu.VMEM((2, TILE, COLS), jnp.float32),
-            pltpu.SMEM((1,), jnp.int32),
-            pltpu.SMEM((1,), jnp.float32),
             pltpu.SemaphoreType.DMA,
-            pltpu.SemaphoreType.DMA((2,)),
+            pltpu.VMEM((2, COLS), jnp.float32),
+            pltpu.SemaphoreType.DMA,
         ],
         compiler_params=grant(FIELD_MIB),
         name="field_away",
@@ -254,13 +250,9 @@
     mine = pl.pallas_call(
         own_kernel,
         out_shape=vmem_f32(HALF, TILE, COLS),
-        in_specs=[smem(), hbm(), hbm(), hbm(), hbm()],
+        in_specs=[smem(), hbm(), hbm(), smem(), hbm()],
         out_specs=vmem(),
-        scratch_shapes=[
-            *gather_scratch,
-            pltpu.SMEM((1,), jnp.int32),
-            pltpu.SemaphoreType.DMA,
-        ],
+        scratch_shapes=gather_scratch,
         compiler_params=grant(FIELD_MIB),
         name="field_own",
     )(tile_of, forward, adjoint, wl_index, fom_sent)

time: 77.5 us -> 77.7 us (level)
  no operation moved by 1% of the time
where the time goes in v3:
time: 77.7 us; the launch traced here: 77.4 us
  blocking collectives  45.5 us (59%)
  Pallas kernels  13.5 us (17%)
  starting transfers between devices  11.7 us (15%)
  waiting for transfers between devices  5.27 us (7%)
  between operations  1.35 us (2%)
    all_to_all x3, blocking collectives, exchanged(): lax.all_to_all(blocks, AXES, 0, 0, tiled=True, axis_index_groups=groups)  45.5 us
    all_to_all x1, starting transfers between devices, exchanged(): lax.all_to_all(blocks, AXES, 0, 0, tiled=True, axis_index_groups=groups)  10.2 us
    pallas_call x1, Pallas kernels, per_device(): pl.pallas_call(away_kernel, out_shape=[vmem_f32(DEVICES, 1, LANES), vmem_...  6.3 us
    all_to_all x1, waiting for transfers between devices, exchanged(): lax.all_to_all(blocks, AXES, 0, 0, tiled=True, axis_index_groups=groups)  5.27 us
    pallas_call x1, Pallas kernels, per_device(): pl.pallas_call(own_kernel, out_shape=vmem_f32(HALF, TILE, COLS), in_specs...  4.4 us
    pallas_call x1, Pallas kernels, per_device(): pl.pallas_call(weigh_kernel, out_shape=vmem_f32(HALF, TILE, COLS), in_spe...  1.78 us
  transfers between devices with their start and end apart: 2, of which 1 were waited for; matrix products, arithmetic and copies ran while one was open for 0% of the time, Pallas kernels for 6%

profile of v3, /device:TPU:1, one launch (start us, length us, event | category | flops | bytes accessed | tf_op | source)
XLA Modules:
  0.0 77.4 jit_solution(1234301533692199376)
XLA Ops:
  1.3 6.3 %field_away.1 = (f32[128,1,128]{2,1,0:T(1,128)}, f32[64,8,1024]{2,1,0:T(8,128)}) custom-call(s32[128]{0:T(128)} %tile_of.3, f32[1,2,1024,1024]{3,2,1,0:T(8,128)} %forward.3, f32[1,2,1024,1024]{3,2,1,0:T(8,128)} %adjoint.3, f32[2,1024]{1,0:T(2,128)} %mode_hbm.1, s32[1]{0:T(128)S(6)} %copy.9.wl_index, f32[1]{0:T(128)S(6)} %copy.8.target), custom_call_target="tpu_custom_call" | custom-call | tf_op jit(solution)/shard_map/field_away/pallas_call | solution.py:233
  7.6 1.5 %collective-permute-start = (f32[64,8,1024]{2,1,0:T(8,128)}, f32[64,8,1024]{2,1,0:T(8,128)}, u32[]{:S(2)}, u32[]{:S(2)}) collective-permute-start(f32[64,8,1024]{2,1,0:T(8,128)} %get-tuple-element.10), channel_id=1, source_target_pairs={{0,4},{4,0},{1,5},{5,1},{2,6},{6,2},{3,7},{7,3},{8,12},{12,8},{9,1... | collective-permute-start | bytes 6291464 | tf_op jit(solution)/shard_map/ppermute | solution.py:248
  9.1 10.2 %all-to-all-start = ((f32[128,1,128]{2,1,0:T(1,128)}), f32[128,1,128]{2,1,0:T(1,128)S(1)}, u32[]{:S(2)}, u32[]{:S(2)}) async-start(f32[128,1,128]{2,1,0:T(1,128)} %get-tuple-element.9.after), calls=%async_computation | async-start | bytes 131072 | tf_op jit(solution)/shard_map/all_to_all | solution.py:224
  19.3 4.4 %field_own.1.mine = f32[64,8,1024]{2,1,0:T(8,128)S(1)} custom-call(s32[128]{0:T(128)} %tile_of.3, f32[1,2,1024,1024]{3,2,1,0:T(8,128)} %forward.3, f32[1,2,1024,1024]{3,2,1,0:T(8,128)} %adjoint.3, s32[1]{0:T(128)S(6)} %copy.9.wl_index, f32[128,1,128]{2,1,0:T(1,128)} %get-tuple-element.9.after), custom_call_target="tpu_custom_call" | custom-call | tf_op jit(solution)/shard_map/field_own/pallas_call | solution.py:250
  23.7 5.3 %all-to-all-done.foms = f32[128,1,128]{2,1,0:T(1,128)S(1)} async-done(((f32[128,1,128]{2,1,0:T(1,128)}), f32[128,1,128]{2,1,0:T(1,128)S(1)}, u32[]{:S(2)}, u32[]{:S(2)}) %all-to-all-start) | async-done | bytes 65568 | tf_op jit(solution)/shard_map/all_to_all | solution.py:224
  29.0 0.0 collective-permute-done.other_hbm
  29.0 1.8 %weigh.1 = f32[64,8,1024]{2,1,0:T(8,128)S(1)} custom-call(f32[128,1,128]{2,1,0:T(1,128)S(1)} %all-to-all-done.foms, f32[64,8,1024]{2,1,0:T(8,128)S(1)} %field_own.1.mine, f32[64,8,1024]{2,1,0:T(8,128)} %collective-permute-done.other_hbm), custom_call_target="tpu_custom_call" | custom-call | tf_op jit(solution)/shard_map/weigh/pallas_call | solution.py:259
  30.8 22.5 %all_to_all.20 = f32[8,64,1024]{2,1,0:T(8,128)S(1)} all-to-all(f32[8,64,1024]{2,1,0:T(8,128)S(1)} %bitcast.2), channel_id=1, replica_groups={{0,1,8,9,32,33,40,41},{2,3,10,11,34,35,42,43},{16,17,24,25,48,49,56,57}..., dimensions={0} | all-to-all | bytes 4194304 | tf_op jit(solution)/shard_map/all_to_all | solution.py:224
  53.3 0.0 copy-start
  53.3 0.1 reduce_sum.9
  53.4 7.9 %all_to_all.21.arrived = f32[8,8,1024]{2,1,0:T(8,128)S(1)} all-to-all(f32[8,8,1024]{2,1,0:T(8,128)S(1)} %bitcast.3), channel_id=1, replica_groups={{0,3,24,27,96,99,120,123},{1,2,25,26,97,98,121,122},{8,11,16,19,104,107..., dimensions={0} | all-to-all | bytes 524288 | tf_op jit(solution)/shard_map/all_to_all | solution.py:224
  61.3 0.0 copy-done
  61.3 0.2 shape.1
  61.5 15.1 %all_to_all.22.squares = f32[128,1,128]{2,1,0:T(1,128)S(1)} all-to-all(f32[128,1,128]{2,1,0:T(1,128)S(1)} %get-tuple-element.11), channel_id=1, replica_groups=mesh['x'=4,'y'=4,'c'=2,'z'=4] {'x','y','c','z'}, dimensions={0} | all-to-all | bytes 131072 | tf_op jit(solution)/shard_map/all_to_all | solution.py:224
  76.6 0.8 %scale.1 = f32[8,1024]{1,0:T(8,128)} custom-call(f32[128,1,128]{2,1,0:T(1,128)S(1)} %all_to_all.22.squares, f32[8,1024]{1,0:T(8,128)S(1)} %get-tuple-element.12.shaped), custom_call_target="tpu_custom_call" | custom-call | tf_op jit(solution)/shard_map/scale/pallas_call | solution.py:282
Async XLA Ops:
  7.6 21.4 %collective-permute-start = (f32[64,8,1024]{2,1,0:T(8,128)}, f32[64,8,1024]{2,1,0:T(8,128)}, u32[]{:S(2)}, u32[]{:S(2)}) collective-permute-start(f32[64,8,1024]{2,1,0:T(8,128)} %get-tuple-element.10), channel_id=1, source_target_pairs={{0,4},{4,0},{1,5},{5,1},{2,6},{6,2},{3,7},{7,3},{8,12},{12,8},{9,1... | collective-permute-start | bytes 6291464 | tf_op jit(solution)/shard_map/ppermute | solution.py:248
  9.1 19.9 %all-to-all-start = ((f32[128,1,128]{2,1,0:T(1,128)}), f32[128,1,128]{2,1,0:T(1,128)S(1)}, u32[]{:S(2)}, u32[]{:S(2)}) async-start(f32[128,1,128]{2,1,0:T(1,128)} %get-tuple-element.9.after), calls=%async_computation | async-start | bytes 131072 | tf_op jit(solution)/shard_map/all_to_all | solution.py:224
  53.3 8.0 %copy-start = (f32[8,1024]{1,0:T(8,128)S(1)}, f32[8,1024]{1,0:T(8,128)}, u32[]{:S(2)}) copy-start(f32[8,1024]{1,0:T(8,128)} %density.1) | copy-start | bytes 98308
